TPU v7x, 32 devices: a whole 2x2x4 slice. The times are simulated.
32 devices in a mesh: sector: 4 (over y, x), box: 8 (over z, core).
Axes of the slice: x: 2, y: 2, z: 4, core: 2. Of those that a mesh axis runs over, the one named last changes fastest.
Arguments:
- positions: float32 [3, 4, 512, 128], P(None, 'sector', 'box'), may hold values from -0.9 to 0.9
- strengths: float32 [3, 4, 512, 128], P(None, 'sector', 'box'), may hold values from -6 to 6
- counts: int32 [4, 512], P('sector', 'box'), may hold values from 1 to 128
- cross_slot: int32 [4, 2048], P('sector', 'box'), may hold values from 0 to 8191, as said below
- arrive_box: int32 [4, 2048], P('sector', 'box'), may hold values from 0 to 63
- il_source: int32 [4, 512, 16], P('sector', 'box'), may hold values from 0 to 63
- il_class: int32 [4, 512, 16], P('sector', 'box'), may hold values from 0 to 3
- m2m: bfloat16 [4, 441, 441], replicated, may hold values from -0.125 to 0.125
- m2l_leaf: bfloat16 [4, 441, 441], replicated, may hold values from -0.0625 to 0.0625
- tree_up: bfloat16 [2, 441, 441], replicated, may hold values from -0.21875 to 0.21875
- tree_m2l: bfloat16 [2, 441, 441], replicated, may hold values from -0.25 to 0.25
- m2l_sector: bfloat16 [3, 441, 441], replicated, may hold values from -0.15625 to 0.15625
Outputs:
- new_positions: float32 [3, 4, 512, 128], P(None, 'sector', 'box')
- velocity: float32 [3, 4, 512, 128], P(None, 'sector', 'box')
Inputs may be any that keep to these rules, and one draw needn't show every extreme that they name: `cross_slot`: within one block's 256 entries the slot numbers are distinct; a slot beyond its box's count carries nothing.
All inputs are finite; a program needn't handle non-finite values.
Results may differ from a plain program's by a relative error of at most 0.006.
Values may be sent and summed in bfloat16 or wider, within the bound.
No kernel may reach another device: no remote copies, remote signals or barrier semaphores. Data moves between devices by JAX's collectives and lax.ppermute only.
A program may use at most 128 MiB of HBM per device.

v0:
```python
import math

import jax
import jax.numpy as jnp
from jax import lax
from jax.sharding import PartitionSpec as P

TERMS = 21
LEVELS_DEV = 3
NCLASS = 4


DELTA_SQ = 0.25
TIME_STEP = 0.02
INV_FOUR_PI = 1.0 / (4.0 * math.pi)
HIGHEST_PRECISION = lax.Precision.HIGHEST
OFFSETS = ((0.0, 0.0, 0.0), (0.0, 0.0, -2.0), (0.0, 0.0, 2.0), (-2.0, 0.0, 0.0), (2.0, 0.0, 0.0))


def with_halo(array, sides, width, wrap):
    for axis, dim in sides:
        devices, length = (lax.axis_size(axis), array.shape[dim])
        up = [(i, (i + 1) % devices) for i in range(devices if wrap else devices - 1)]
        down = [(j, i) for i, j in up]
        last = lax.slice_in_dim(array, length - width, length, axis=dim)
        first = lax.slice_in_dim(array, 0, width, axis=dim)
        before = lax.ppermute(last, axis, up)
        after = lax.ppermute(first, axis, down)
        array = jnp.concatenate([before, array, after], axis=dim)
    return array


def partner_2(block, axis, distance):
    count = lax.axis_size(axis)
    route = []
    for low in range(count):
        high = low | 1 << distance
        if high != low and high < count:
            route += [(low, high), (high, low)]
    return lax.ppermute(block, axis, route)


def passed_along(array, axis, by):
    devices = lax.axis_size(axis)
    return lax.ppermute(array, axis, [(i, (i + by) % devices) for i in range(devices)])


def chebyshev(coordinate):
    scaled = 0.5 * coordinate
    series = [jnp.ones_like(scaled), scaled]
    for order in range(2, TERMS):
        series.append(2.0 * scaled * series[-1] - series[-2])
    return jnp.stack(series[:TERMS])


def multipoles(cheb_a, cheb_b, weights):
    weighted = weights[:, None] * cheb_a[None]
    return jnp.einsum("cjnp,knp->ncjk", weighted, cheb_b, precision=HIGHEST_PRECISION)


def evaluate(local, cheb_a, cheb_b):
    shaped = local.reshape(local.shape[0], 3, TERMS, TERMS)
    partial_sum = jnp.einsum("ncjk,knp->cjnp", shaped, cheb_b, precision=HIGHEST_PRECISION)
    return jnp.sum(partial_sum * cheb_a[None], axis=1) / TERMS


def pair_velocity(target, source, weight, offset):
    delta_x = target[0][:, :, None] - (source[0][:, None, :] + offset[0])
    delta_y = target[1][:, :, None] - (source[1][:, None, :] + offset[1])
    delta_z = target[2][:, :, None] - (source[2][:, None, :] + offset[2])
    radius_sq = delta_x * delta_x + delta_y * delta_y + delta_z * delta_z + DELTA_SQ
    inverse = INV_FOUR_PI / (radius_sq * jnp.sqrt(radius_sq))
    weight_x = weight[0][:, None, :]
    weight_y = weight[1][:, None, :]
    weight_z = weight[2][:, None, :]
    speed_x = jnp.sum(inverse * (weight_y * delta_z - weight_z * delta_y), axis=2)
    speed_y = jnp.sum(inverse * (weight_z * delta_x - weight_x * delta_z), axis=2)
    speed_z = jnp.sum(inverse * (weight_x * delta_y - weight_y * delta_x), axis=2)
    return jnp.stack([speed_x, speed_y, speed_z])


def near_field(places, weights):
    box_count, slots = (places.shape[1], places.shape[2])
    stacked = jnp.concatenate([places, weights], axis=0)[:, None]
    beside = with_halo(stacked.astype(jnp.bfloat16), (("sector", 1),), 1, True).astype(
        stacked.dtype
    )
    along = with_halo(stacked.astype(jnp.bfloat16), (("box", 2),), 1, False).astype(stacked.dtype)
    sources = [stacked[:, 0], along[:, 0, :box_count], along[:, 0, 2:], beside[:, 0], beside[:, 2]]
    block = math.gcd(box_count, 64)
    block_count = box_count // block

    def arrange(array):
        return array.reshape(array.shape[0], block_count, block, slots).transpose(1, 0, 2, 3)

    inputs = (arrange(places),) + tuple((arrange(item) for item in sources))

    def block_velocity(items):
        summed = jnp.zeros_like(items[0])
        for index in range(5):
            summed = summed + pair_velocity(
                items[0], items[1 + index][:3], items[1 + index][3:], OFFSETS[index]
            )
        return summed

    result = lax.map(block_velocity, inputs)
    return result.transpose(1, 0, 2, 3).reshape(3, box_count, slots)


def merge_pair(current, partner, side_bit, tree_up):
    lower_node = jnp.where(side_bit == 0, current, partner)
    upper_node = jnp.where(side_bit == 0, partner, current)
    merged = jnp.dot(lower_node, tree_up[0], preferred_element_type=jnp.float32) + jnp.dot(
        upper_node, tree_up[1], preferred_element_type=jnp.float32
    )
    return merged.astype(jnp.bfloat16)


def far_field(
    places,
    weights,
    arrival_terms,
    il_source,
    il_class,
    m2m,
    m2l_leaf,
    tree_up,
    tree_m2l,
    m2l_sector,
):
    box_count = places.shape[1]
    coef = TERMS * TERMS
    cheb_a = chebyshev(places[0])
    cheb_b = chebyshev(places[1])
    leaf = (
        (multipoles(cheb_a, cheb_b, weights) + arrival_terms)
        .reshape(box_count, 3, coef)
        .astype(jnp.bfloat16)
    )
    upward = leaf
    for depth in range(LEVELS_DEV):
        grouped = upward.reshape(-1, 4, 3, coef)
        upward = jnp.einsum(
            "gocx,oxy->gcy", grouped, m2m, preferred_element_type=jnp.float32
        ).astype(jnp.bfloat16)
    block_root = upward[0]
    box_index = lax.axis_index("box")
    depth_count = lax.axis_size("box").bit_length() - 1
    siblings = []
    side_bits = []
    current = block_root
    for depth in range(depth_count):
        partner = partner_2(current, "box", depth)
        side_bit = box_index >> depth & 1
        siblings.append(partner)
        side_bits.append(side_bit)
        current = merge_pair(current, partner, side_bit, tree_up)
    sector_index = lax.axis_index("sector")
    sector_count = lax.axis_size("sector")
    piece = lax.all_gather(current[None], "sector", axis=0, tiled=True)
    source_ids = jnp.arange(piece.shape[0], dtype=jnp.int32)
    distance = (source_ids - sector_index) % sector_count
    matrices = m2l_sector[jnp.maximum(distance - 1, 0)]
    masked_piece = jnp.where((distance != 0)[:, None, None], piece, jnp.zeros_like(piece))
    far_sum = jnp.einsum("ncx,nxy->cy", masked_piece, matrices, preferred_element_type=jnp.float32)
    local = far_sum.astype(jnp.bfloat16)
    for depth in reversed(range(depth_count)):
        up_side = lax.dynamic_index_in_dim(tree_up, side_bits[depth], 0, keepdims=False)
        cross_side = lax.dynamic_index_in_dim(tree_m2l, side_bits[depth], 0, keepdims=False)
        downward = jnp.einsum(
            "cy,xy->cx", local, up_side, preferred_element_type=jnp.float32
        ) + jnp.dot(siblings[depth], cross_side, preferred_element_type=jnp.float32)
        local = downward.astype(jnp.bfloat16)
    parent_local = local[None]
    child = jnp.zeros((box_count, 3, coef), jnp.float32)
    for depth in range(LEVELS_DEV):
        child = jnp.einsum(
            "gcy,oxy->gocx", parent_local, m2m, preferred_element_type=jnp.float32
        ).reshape(-1, 3, coef)
        if depth + 1 < LEVELS_DEV:
            parent_local = child.astype(jnp.bfloat16)
    box_ids = jnp.arange(box_count, dtype=jnp.int32)
    source_hit = (il_source[0][:, :, None] == box_ids[None, None, :]).astype(jnp.bfloat16)
    class_hit = (
        il_class[0][:, :, None] == jnp.arange(NCLASS, dtype=jnp.int32)[None, None, :]
    ).astype(jnp.bfloat16)
    pair_counts = jnp.einsum(
        "bic,bis->cbs", class_hit, source_hit, preferred_element_type=jnp.float32
    ).astype(jnp.bfloat16)
    presum = jnp.einsum(
        "cbs,sx->cbx",
        pair_counts,
        leaf.reshape(box_count, 3 * coef),
        preferred_element_type=jnp.float32,
    )
    presum = presum.astype(jnp.bfloat16).reshape(NCLASS, box_count * 3, coef)
    translated = jnp.einsum(
        "cnx,cxy->ny", presum, m2l_leaf, preferred_element_type=jnp.float32
    ).reshape(box_count, 3, coef)
    return evaluate(child + translated, cheb_a, cheb_b)


def per_device(
    positions,
    strengths,
    counts,
    cross_slot,
    arrive_box,
    il_source,
    il_class,
    m2m,
    m2l_leaf,
    tree_up,
    tree_m2l,
    m2l_sector,
):
    box_count, slots = (positions.shape[2], positions.shape[3])
    slot_ids = jnp.arange(slots, dtype=jnp.int32)
    present = (slot_ids[None, :] < counts[0][:, None]).astype(jnp.float32)
    crossing = cross_slot[0]
    departed = jnp.zeros((box_count * slots,), jnp.float32).at[crossing].set(1.0)
    live = present * (1.0 - departed.reshape(box_count, slots))
    flat_places = positions[:, 0].reshape(3, box_count * slots)
    flat_strength = strengths[:, 0].reshape(3, box_count * slots)
    leave_present = present.reshape(-1)[crossing]
    leaving = jnp.concatenate(
        [flat_places[:, crossing], flat_strength[:, crossing] * leave_present[None]], axis=0
    )
    arrived = passed_along(leaving, "sector", 1)
    arrive_cheb_a = chebyshev(arrived[0][:, None])
    arrive_cheb_b = chebyshev(arrived[1][:, None])
    arrival_each = multipoles(arrive_cheb_a, arrive_cheb_b, arrived[3:6][:, :, None])
    box_ids = jnp.arange(box_count, dtype=jnp.int32)
    landing = (arrive_box[0][None, :] == box_ids[:, None]).astype(jnp.float32)
    arrival_terms = jnp.dot(
        landing, arrival_each.reshape(landing.shape[1], -1), precision=HIGHEST_PRECISION
    )
    arrival_terms = arrival_terms.reshape(box_count, 3, TERMS, TERMS)
    places = positions[:, 0]
    weights = strengths[:, 0] * live[None]
    velocity = jnp.zeros_like(places)
    for substep in range(2):
        near = near_field(places, weights)
        far = far_field(
            places,
            weights,
            arrival_terms,
            il_source,
            il_class,
            m2m,
            m2l_leaf,
            tree_up,
            tree_m2l,
            m2l_sector,
        )
        velocity = near + far
        places = places + TIME_STEP * velocity
    return (places[:, None], velocity[:, None])


def solution(mesh):
    placed = (
        P(None, "sector", "box", None),
        P(None, "sector", "box", None),
        P("sector", "box"),
        P("sector", "box"),
        P("sector", "box"),
        P("sector", "box", None),
        P("sector", "box", None),
        P(),
        P(),
        P(),
        P(),
        P(),
    )
    return jax.shard_map(
        per_device,
        mesh=mesh,
        in_specs=placed,
        out_specs=(P(None, "sector", "box", None), P(None, "sector", "box", None)),
        check_vma=False,
    )
```

profile of v0, /device:TPU:0, one launch (start us, length us, event | category | flops | bytes accessed | tf_op | source)
XLA Modules:
  0.0 347.4 jit_solution(13290622391281535371)
XLA Ops:
  6.8 3.9 %collective-permute-start.3 = (bf16[6,1,64,128]{3,2,1,0:T(8,128)(2,1)}, bf16[6,1,64,128]{3,2,1,0:T(8,128)(2,1)}, u32[]{:S(2)}, u32[]{:S(2)}) collective-permute-start(bf16[6,1,64,128]{3,2,1,0:T(8,128)(2,1)} %get-tuple-element.194), channel_id=1, source_target_pairs={{8,0},{16,8},{24,16},{0,24},{9,1},{17,9},{25,17},{1,25},{10,2},{18... | collective-permute-start | bytes 294920 | tf_op jit(solution)/shard_map/ppermute | solution.py:28
  10.8 3.4 copy.318
  17.0 3.0 gather_fusion.1
  21.9 2.9 gather_fusion
  28.8 3.0 collective-permute-start
  49.5 5.8 %constant_dynamic-slice_fusion.1 = (bf16[1,441,441]{2,0,1:T(2,128)(2,1)}, bf16[1,441,441]{2,0,1:T(2,128)(2,1)}, bf16[1,441,441]{2,0,1:T(2,128)(2,1)}, bf16[1,441,441]{2,0,1:T(2,128)(2,1)}, bf16[1,441,441]{2,0,1:T(2,128)(2,1)}) fusion(bf16[2,441,441]{2,0,1:T(2,128)(2,1)S(1)} %copy-done.4, s32[]{:T(128)S(6)} %select_n.134, s32[]{:T(128)S(6)} %select_n.133, ...), kind=kLoop, calls=%fused_computation.792 | loop fusion | bytes 3889632 | tf_op jit(solution)/shard_map/jit(dynamic_index_in_dim)/dynamic_slice | solution.py:168
  55.4 4.1 %constant_dynamic-slice_fusion = (bf16[1,441,441]{2,0,1:T(2,128)(2,1)}, bf16[1,441,441]{2,0,1:T(2,128)(2,1)}, bf16[1,441,441]{2,0,1:T(2,128)(2,1)}) fusion(bf16[2,441,441]{2,0,1:T(2,128)(2,1)S(1)} %copy-done.5, s32[]{:T(128)S(6)} %select_n.134, s32[]{:T(128)S(6)} %select_n.133, s32[]{:T(128)S(6)} %select_n.132), kind=kLoop, calls=%fused_computation.791 | loop fusion | bytes 2333784 | tf_op jit(solution)/shard_map/jit(dynamic_index_in_dim)/dynamic_slice | solution.py:169
  62.9 6.8 %fusion.134 = f32[64,3,21,21]{3,2,1,0:T(8,128)} fusion(f32[21,64,128]{2,0,1:T(8,128)} %copy.315, f32[3,64,128]{2,0,1:T(4,128)S(1)} %copy.314, f32[21,64,128,1]{2,1,0,3:T(8,128)} %bitcast.1373), kind=kOutput, calls=%fused_computation.243 | convolution fusion | flops 130572288 | bytes 1813248 | tf_op jit(solution)/shard_map/cjnp,knp->ncjk/dot_general | solution.py:58
  70.3 3.2 copy.321
  78.8 2.8 dot_general.169
  81.6 3.5 add_convert_fusion.1
  98.9 25.5 %fusion.45 = (f32[64,128]{1,0:T(8,128)S(1)}, f32[64,128]{1,0:T(8,128)}, f32[64,128]{1,0:T(8,128)}, f32[64,128]{1,0:T(8,128)}, f32[64,128]{1,0:T(8,128)}, /*index=5*/f32[64,128]{1,0:T(8,128)}) fusion(f32[64,128]{1,0:T(8,128)S(1)} %get-tuple-element.164, f32[64,128]{1,0:T(8,128)S(1)} %get-tuple-element.165, f32[64,128]{1,0:T(8,128)S(1)} %get-tuple-element.166, ...), kind=kLoop, calls=%fused_computation.150 | loop fusion | flops 54476800 | bytes 688128 | tf_op jit(solution)/shard_map/while/body/eval_jaxpr/reduce_sum | solution.py:76
  137.3 9.0 %all-gather.2 = bf16[4,3,441]{2,1,0:T(4,128)(2,1)} all-gather(bf16[1,3,441]{2,1,0:T(4,128)(2,1)S(1)} %fusion.258), channel_id=2, replica_groups=mesh['sector'=4,'box'=8] {'sector'}, dimensions={0}, use_global_device_ids=true | all-gather | bytes 13230 | tf_op jit(solution)/shard_map/all_gather | solution.py:160
  146.3 3.0 fusion.260
  168.0 3.3 reshape.4930
  171.4 6.1 %fusion.131 = f32[3,64,128]{2,0,1:T(4,128)S(1)} fusion(f32[64,3,21,21]{3,2,1,0:T(8,128)} %reshape.4930, f32[21,64,128]{2,0,1:T(8,128)} %copy.315, f32[21,64,128,1]{2,1,0,3:T(8,128)} %bitcast.1374), kind=kOutput, calls=%fused_computation.240 | convolution fusion | flops 131063808 | bytes 1813248 | tf_op jit(solution)/shard_map/ncjk,knp->cjnp/dot_general | solution.py:63
  178.9 29.2 %fusion.69 = (f32[64,128]{1,0:T(8,128)S(1)}, f32[64,128]{1,0:T(8,128)S(1)}, f32[64,128]{1,0:T(8,128)S(1)}, f32[64,128]{1,0:T(8,128)S(1)}, f32[64,128]{1,0:T(8,12...) fusion(f32[64,128]{1,0:T(8,128)S(1)} %get-tuple-element.140, ...), kind=kLoop, calls=%fused_computation.174 | loop fusion | flops 81715200 | bytes 884736 | tf_op jit(solution)/shard_map/while/body/eval_jaxpr/reduce_sum | solution.py:76
  212.2 5.5 %fusion.132 = f32[64,3,21,21]{3,2,1,0:T(8,128)} fusion(f32[21,64,128]{2,0,1:T(8,128)S(1)} %copy.354, f32[3,64,128]{2,0,1:T(4,128)S(1)} %copy-done.11, f32[21,64,128,1]{2,1,0,3:T(8,128)S(1)} %bitcast.1371), kind=kOutput, calls=%fused_computation.241 | convolution fusion | flops 130572288 | bytes 1813248 | tf_op jit(solution)/shard_map/cjnp,knp->ncjk/dot_general | solution.py:58
  217.6 3.2 copy.356
  244.1 3.0 collective-permute-start.8
  261.0 25.5 %fusion.105 = (f32[64,128]{1,0:T(8,128)S(1)}, f32[64,128]{1,0:T(8,128)}, f32[64,128]{1,0:T(8,128)}, f32[64,128]{1,0:T(8,128)}, f32[64,128]{1,0:T(8,128)}, /*index=5*/f32[64,128]{1,0:T(8,128)}) fusion(f32[64,128]{1,0:T(8,128)S(1)} %get-tuple-element.152, f32[64,128]{1,0:T(8,128)S(1)} %get-tuple-element.153, f32[64,128]{1,0:T(8,128)S(1)} %get-tuple-element.154, ...), kind=kLoop, calls=%fused_computation.210 | loop fusion | flops 54476800 | bytes 688128 | tf_op jit(solution)/shard_map/while/body/eval_jaxpr/reduce_sum | solution.py:76
  286.9 8.3 %all-gather.3 = bf16[4,3,441]{2,1,0:T(4,128)(2,1)S(1)} all-gather(bf16[1,3,441]{2,1,0:T(4,128)(2,1)S(1)} %fusion.256), channel_id=3, replica_groups=mesh['sector'=4,'box'=8] {'sector'}, dimensions={0}, use_global_device_ids=true | all-gather | bytes 13230 | tf_op jit(solution)/shard_map/all_gather | solution.py:160
  310.5 5.9 %fusion.130 = f32[3,64,128]{2,0,1:T(4,128)S(1)} fusion(f32[64,3,21,21]{3,2,1,0:T(8,128)} %reshape.4932, f32[21,64,128]{2,0,1:T(8,128)S(1)} %copy-done.7, f32[21,64,128,1]{2,1,0,3:T(8,128)S(1)} %bitcast.1372), kind=kOutput, calls=%fused_computation.238 | convolution fusion | flops 131063808 | bytes 1813248 | tf_op jit(solution)/shard_map/ncjk,knp->cjnp/dot_general | solution.py:63
  317.6 28.9 %fusion.129 = (f32[64,128]{1,0:T(8,128)S(1)}, f32[64,128]{1,0:T(8,128)S(1)}, f32[64,128]{1,0:T(8,128)S(1)}, f32[64,128]{1,0:T(8,128)S(1)}, f32[64,128]{1,0:T(8,1...) fusion(f32[64,128]{1,0:T(8,128)S(1)} %get-tuple-element.128, ...), kind=kLoop, calls=%fused_computation.234 | loop fusion | flops 81715200 | bytes 884736 | tf_op jit(solution)/shard_map/while/body/eval_jaxpr/reduce_sum | solution.py:76
  (369 shorter events, 146.2 us)
Async XLA Ops:
  0.6 72.9 %copy-start = (bf16[3,441,441]{2,1,0:T(8,128)(2,1)S(1)}, bf16[3,441,441]{2,1,0:T(8,128)(2,1)}, u32[]{:S(2)}) copy-start(bf16[3,441,441]{2,1,0:T(8,128)(2,1)} %param.23) | copy-start | bytes 3500662
  6.8 170.8 %collective-permute-start.3 = (bf16[6,1,64,128]{3,2,1,0:T(8,128)(2,1)}, bf16[6,1,64,128]{3,2,1,0:T(8,128)(2,1)}, u32[]{:S(2)}, u32[]{:S(2)}) collective-permute-start(bf16[6,1,64,128]{3,2,1,0:T(8,128)(2,1)} %get-tuple-element.194), channel_id=1, source_target_pairs={{8,0},{16,8},{24,16},{0,24},{9,1},{17,9},{25,17},{1,25},{10,2},{18... | collective-permute-start | bytes 294920 | tf_op jit(solution)/shard_map/ppermute | solution.py:28
  10.8 166.9 %collective-permute-start.2 = (bf16[6,1,64,128]{3,2,1,0:T(8,128)(2,1)}, bf16[6,1,64,128]{3,2,1,0:T(8,128)(2,1)}, u32[]{:S(2)}, u32[]{:S(2)}) collective-permute-start(bf16[6,1,64,128]{3,2,1,0:T(8,128)(2,1)} %get-tuple-element.194), channel_id=1, source_target_pairs={{0,8},{8,16},{16,24},{24,0},{1,9},{9,17},{17,25},{25,1},{2,10},{10... | collective-permute-start | bytes 294920 | tf_op jit(solution)/shard_map/ppermute | solution.py:27
  17.0 32.5 %copy-start.4 = (bf16[2,441,441]{2,0,1:T(2,128)(2,1)S(1)}, bf16[2,441,441]{2,0,1:T(2,128)(2,1)}, u32[]{:S(2)}) copy-start(bf16[2,441,441]{2,0,1:T(2,128)(2,1)} %param.21) | copy-start | bytes 2333776
  24.9 51.3 %collective-permute-start.4 = (f32[6,256]{1,0:T(8,128)S(1)}, f32[6,256]{1,0:T(8,128)S(1)}, u32[]{:S(2)}, u32[]{:S(2)}) collective-permute-start(f32[6,256]{1,0:T(8,128)S(1)} %pad_maximum_fusion.6), channel_id=1, source_target_pairs={{0,8},{8,16},{16,24},{24,0},{1,9},{9,17},{17,25},{25,1},{2,10},{10... | collective-permute-start | bytes 18440 | tf_op jit(solution)/shard_map/ppermute | solution.py:45
  27.5 47.9 %collective-permute-start.1 = (bf16[6,1,1,128]{3,2,0,1:T(2,128)(2,1)}, bf16[6,1,1,128]{3,2,0,1:T(2,128)(2,1)S(1)}, u32[]{:S(2)}, u32[]{:S(2)}) collective-permute-start(bf16[6,1,1,128]{3,2,0,1:T(2,128)(2,1)} %get-tuple-element.190), channel_id=1, source_target_pairs={{1,0},{2,1},{3,2},{4,3},{5,4},{6,5},{7,6},{9,8},{10,9},{11,10},{12... | collective-permute-start | bytes 4616 | tf_op jit(solution)/shard_map/ppermute | solution.py:28
  28.8 46.6 %collective-permute-start = (bf16[6,1,1,128]{3,2,0,1:T(2,128)(2,1)S(1)}, bf16[6,1,1,128]{3,2,0,1:T(2,128)(2,1)S(1)}, u32[]{:S(2)}, u32[]{:S(2)}) collective-permute-start(bf16[6,1,1,128]{3,2,0,1:T(2,128)(2,1)S(1)} %get-tuple-element.189), channel_id=1, source_target_pairs={{0,1},{1,2},{2,3},{3,4},{4,5},{5,6},{6,7},{8,9},{9,10},{10,11},{11... | collective-permute-start | bytes 4616 | tf_op jit(solution)/shard_map/ppermute | solution.py:27
  94.8 2.2 collective-permute-start.5
  97.3 29.0 %collective-permute-start.6 = (bf16[3,441]{1,0:T(4,128)(2,1)S(1)}, bf16[3,441]{1,0:T(4,128)(2,1)S(1)}, u32[]{:S(2)}, u32[]{:S(2)}) collective-permute-start(bf16[3,441]{1,0:T(4,128)(2,1)S(1)} %fusion.239), channel_id=1, source_target_pairs={{0,2},{2,0},{1,3},{3,1},{4,6},{6,4},{5,7},{7,5},{8,10},{10,8},{9,1... | collective-permute-start | bytes 7946 | tf_op jit(solution)/shard_map/ppermute | solution.py:40
  127.2 9.0 %collective-permute-start.7 = (bf16[3,441]{1,0:T(4,128)(2,1)}, bf16[3,441]{1,0:T(4,128)(2,1)S(1)}, u32[]{:S(2)}, u32[]{:S(2)}) collective-permute-start(bf16[3,441]{1,0:T(4,128)(2,1)} %fusion.240), channel_id=1, source_target_pairs={{0,4},{4,0},{1,5},{5,1},{2,6},{6,2},{3,7},{7,3},{8,12},{12,8},{9,1... | collective-permute-start | bytes 7946 | tf_op jit(solution)/shard_map/ppermute | solution.py:40
  177.5 31.4 %copy-start.12 = (f32[3,64,128]{2,0,1:T(4,128)}, f32[3,64,128]{2,0,1:T(4,128)S(1)}, u32[]{:S(2)}) copy-start(f32[3,64,128]{2,0,1:T(4,128)S(1)} %fusion.131) | copy-start | bytes 294916
  177.6 30.6 %copy-start.24 = (f32[64,128]{1,0:T(8,128)S(1)}, f32[64,128]{1,0:T(8,128)}, u32[]{:S(2)}) copy-start(f32[64,128]{1,0:T(8,128)} %get-tuple-element.81) | copy-start | bytes 98308
  177.6 30.6 %copy-start.25 = (f32[64,128]{1,0:T(8,128)S(1)}, f32[64,128]{1,0:T(8,128)}, u32[]{:S(2)}) copy-start(f32[64,128]{1,0:T(8,128)} %get-tuple-element.82) | copy-start | bytes 98308
  177.6 31.3 %copy-start.16 = (f32[21,64,128]{2,1,0:T(8,128)S(1)}, f32[21,64,128]{2,1,0:T(8,128)}, u32[]{:S(2)}) copy-start(f32[21,64,128]{2,1,0:T(8,128)} %get-tuple-element.216) | copy-start | bytes 2064388
  178.9 33.3 %copy-start.11 = (f32[3,64,128]{2,0,1:T(4,128)S(1)}, f32[3,64,128]{2,0,1:T(4,128)}, u32[]{:S(2)}) copy-start(f32[3,64,128]{2,0,1:T(4,128)} %copy-done.10) | copy-start | bytes 294916
  230.8 85.7 %collective-permute-start.11 = (bf16[6,1,64,128]{3,2,1,0:T(8,128)(2,1)}, bf16[6,1,64,128]{3,2,1,0:T(8,128)(2,1)}, u32[]{:S(2)}, u32[]{:S(2)}) collective-permute-start(bf16[6,1,64,128]{3,2,1,0:T(8,128)(2,1)} %pad_maximum_fusion.2), channel_id=1, source_target_pairs={{8,0},{16,8},{24,16},{0,24},{9,1},{17,9},{25,17},{1,25},{10,2},{18... | collective-permute-start | bytes 294920 | tf_op jit(solution)/shard_map/ppermute | solution.py:28
  232.2 84.3 %collective-permute-start.10 = (bf16[6,1,64,128]{3,2,1,0:T(8,128)(2,1)}, bf16[6,1,64,128]{3,2,1,0:T(8,128)(2,1)}, u32[]{:S(2)}, u32[]{:S(2)}) collective-permute-start(bf16[6,1,64,128]{3,2,1,0:T(8,128)(2,1)} %pad_maximum_fusion.2), channel_id=1, source_target_pairs={{0,8},{8,16},{16,24},{24,0},{1,9},{9,17},{17,25},{25,1},{2,10},{10... | collective-permute-start | bytes 294920 | tf_op jit(solution)/shard_map/ppermute | solution.py:27
  240.6 13.5 %collective-permute-start.12 = (bf16[3,441]{1,0:T(4,128)(2,1)S(1)}, bf16[3,441]{1,0:T(4,128)(2,1)S(1)}, u32[]{:S(2)}, u32[]{:S(2)}) collective-permute-start(bf16[3,441]{1,0:T(4,128)(2,1)S(1)} %fusion.236), channel_id=1, source_target_pairs={{0,1},{1,0},{2,3},{3,2},{4,5},{5,4},{6,7},{7,6},{8,9},{9,8},{10,11... | collective-permute-start | bytes 7946 | tf_op jit(solution)/shard_map/ppermute | solution.py:40
  242.9 10.3 %collective-permute-start.9 = (bf16[6,1,1,128]{3,2,1,0:T(2,128)(2,1)S(1)}, bf16[6,1,1,128]{3,2,1,0:T(2,128)(2,1)S(1)}, u32[]{:S(2)}, u32[]{:S(2)}) collective-permute-start(bf16[6,1,1,128]{3,2,1,0:T(2,128)(2,1)S(1)} %get-tuple-element.177), channel_id=1, source_target_pairs={{1,0},{2,1},{3,2},{4,3},{5,4},{6,5},{7,6},{9,8},{10,9},{11,10},{12... | collective-permute-start | bytes 4616 | tf_op jit(solution)/shard_map/ppermute | solution.py:28
  244.1 9.0 %collective-permute-start.8 = (bf16[6,1,1,128]{3,2,1,0:T(2,128)(2,1)S(1)}, bf16[6,1,1,128]{3,2,1,0:T(2,128)(2,1)S(1)}, u32[]{:S(2)}, u32[]{:S(2)}) collective-permute-start(bf16[6,1,1,128]{3,2,1,0:T(2,128)(2,1)S(1)} %get-tuple-element.176), channel_id=1, source_target_pairs={{0,1},{1,2},{2,3},{3,4},{4,5},{5,6},{6,7},{8,9},{9,10},{10,11},{11... | collective-permute-start | bytes 4616 | tf_op jit(solution)/shard_map/ppermute | solution.py:27
  253.2 42.0 %copy-start.59 = (pred[4]{0:T(512)(128)(4,1)S(1)}, pred[4]{0:T(512)(128)(4,1)}, u32[]{:S(2)}) copy-start(pred[4]{0:T(512)(128)(4,1)} %fusion.418) | copy-start | bytes 16
  254.5 3.6 %collective-permute-start.13 = (bf16[3,441]{1,0:T(4,128)(2,1)S(1)}, bf16[3,441]{1,0:T(4,128)(2,1)S(1)}, u32[]{:S(2)}, u32[]{:S(2)}) collective-permute-start(bf16[3,441]{1,0:T(4,128)(2,1)S(1)} %fusion.245), channel_id=1, source_target_pairs={{0,2},{2,0},{1,3},{3,1},{4,6},{6,4},{5,7},{7,5},{8,10},{10,8},{9,1... | collective-permute-start | bytes 7946 | tf_op jit(solution)/shard_map/ppermute | solution.py:40
  258.4 28.1 %collective-permute-start.14 = (bf16[3,441]{1,0:T(4,128)(2,1)S(1)}, bf16[3,441]{1,0:T(4,128)(2,1)S(1)}, u32[]{:S(2)}, u32[]{:S(2)}) collective-permute-start(bf16[3,441]{1,0:T(4,128)(2,1)S(1)} %fusion.246), channel_id=1, source_target_pairs={{0,4},{4,0},{1,5},{5,1},{2,6},{6,2},{3,7},{7,3},{8,12},{12,8},{9,1... | collective-permute-start | bytes 7946 | tf_op jit(solution)/shard_map/ppermute | solution.py:40
  310.5 36.7 %copy-start.1 = (bf16[3,441,441]{2,1,0:T(8,128)(2,1)S(1)}, bf16[3,441,441]{2,1,0:T(8,128)(2,1)}, u32[]{:S(2)}) copy-start(bf16[3,441,441]{2,1,0:T(8,128)(2,1)} %param.23) | copy-start | bytes 3500662
  (51 other events, 595.1 us)
where the time goes:
time: 353 us; the launch traced here: 347 us
  other arithmetic  144 us (41%)
  local copies, waits for them, and re-layouts  85.4 us (24%)
  matrix products  71.1 us (20%)
  starting transfers between devices  25.2 us (7%)
  blocking collectives  17.3 us (5%)
    reduce_sum x4, other arithmetic, pair_velocity(): jnp.sum(inverse * (weight_y * delta_z - weight_z * delta_y), axis=2)  109 us
    all_gather x2, blocking collectives, far_field(): piece = lax.all_gather(current[None], 'sector', axis=0, tiled=True)  17.3 us
    convert_element_type x6, local copies, waits for them, and re-layouts, far_field(): leaf = (multipoles(cheb_a, cheb_b, weights) + arrival_terms).reshape(box_...  14.5 us
    unnamed x105, other arithmetic  14.2 us
    dot_general x6, matrix products, far_field(): jnp.einsum('cy,xy->cx', local, up_side, preferred_element_type=jnp.float32)  13.6 us
    dot_general x2, matrix products, multipoles(): jnp.einsum('cjnp,knp->ncjk', weighted, cheb_b, precision=HIGHEST_PRECISION)  12.3 us
    dot_general x2, matrix products, evaluate(): jnp.einsum('ncjk,knp->cjnp', shaped, cheb_b, precision=HIGHEST_PRECISION)  12 us
    reshape x4, local copies, waits for them, and re-layouts, far_field(): presum = presum.astype(jnp.bfloat16).reshape(NCLASS, box_count * 3, coef)  10.6 us
  transfers between devices with their start and end apart: 15, of which 1 were waited for; matrix products, arithmetic and copies ran while one was open for 61% of the time, Pallas kernels for 0%

commit v1 on v0

v1 whole, which is shorter than its diff:
```python
import functools
import math

import jax
import jax.numpy as jnp
from jax import lax
from jax.experimental import pallas as pl
from jax.experimental.pallas import tpu as pltpu
from jax.sharding import PartitionSpec as P

TERMS = 21
TERMS_PAD = 24
LEVELS_DEV = 3
NCLASS = 4
COMP_PAD = 4

DELTA_SQ = 0.25
TIME_STEP = 0.02
INV_FOUR_PI = 1.0 / (4.0 * math.pi)
OFFSETS = ((0.0, 0.0, 0.0), (0.0, 0.0, -2.0), (0.0, 0.0, 2.0), (-2.0, 0.0, 0.0), (2.0, 0.0, 0.0))
PIECES = 16
F32 = jnp.float32
BF16 = jnp.bfloat16
NN = (((1,), (0,)), ((), ()))
NT = (((1,), (1,)), ((), ()))
TN = (((0,), (0,)), ((), ()))


def rounded(value):
    return value.astype(BF16).astype(F32)


def matmul(left, right, dims=NN):
    return lax.dot_general(left, right, dims, preferred_element_type=F32)


def digit_reversed(value):
    out = value & 3
    for level in range(1, LEVELS_DEV):
        out = out * 4 + (lax.shift_right_logical(value, 2 * level) & 3)
    return out


def iota(shape, dim):
    return lax.broadcasted_iota(jnp.int32, shape, dim)


def coefficient_spread(coef, wide):
    column = iota((1, coef), 1)
    target = column + (TERMS_PAD - TERMS) * lax.shift_right_logical(column * 3121, 16)
    return (iota((wide, coef), 0) == target).astype(F32).astype(BF16)


def chebyshev_series(coordinate):
    scaled = 0.5 * coordinate
    series = [jnp.ones_like(scaled), scaled]
    for _ in range(2, TERMS):
        series.append(2.0 * scaled * series[-1] - series[-2])
    return series


def fill_chebyshev(ref, coordinate):
    boxes = coordinate.shape[0]
    for order, term in enumerate(chebyshev_series(coordinate)):
        ref[order * boxes : (order + 1) * boxes, :] = term
    ref[TERMS * boxes :, :] = jnp.zeros(((TERMS_PAD - TERMS) * boxes, coordinate.shape[1]), F32)


def outer_terms(cheb_a, cheb_b):
    lanes = cheb_a.shape[1]
    product = (cheb_a[:TERMS, None, :] * cheb_b[None, :, :]).reshape(TERMS * TERMS_PAD, lanes)
    fill = -product.shape[0] % 128
    return jnp.concatenate([product, jnp.zeros((fill, lanes), F32)], axis=0).astype(BF16)


def box_terms(cheb_a_ref, cheb_b_ref, box, boxes):
    rows = pl.ds(box, TERMS_PAD, stride=boxes)
    return outer_terms(cheb_a_ref[rows, :], cheb_b_ref[rows, :])


def high_low(value):
    high = rounded(value)
    return jnp.concatenate([high, value - high], axis=0).astype(BF16)


def leaf_rows(cheb_a_ref, cheb_b_ref, spread_weights_ref, leaf_ref, boxes):
    first = iota((8, 1), 0) < COMP_PAD

    def pair(index, carry):
        rows = pl.ds(pl.multiple_of(index * 8, 8), 8)
        weights = high_low(spread_weights_ref[rows, :])
        summed = []
        for half in range(2):
            box = digit_reversed(index * 2 + half)
            both = matmul(weights, box_terms(cheb_a_ref, cheb_b_ref, box, boxes), NT)
            summed.append(both[:8] + both[8:])
        leaf_ref[rows, :] = jnp.where(first, summed[0], summed[1])
        return carry

    lax.fori_loop(0, boxes // 2, pair, 0, unroll=2)


def upward(leaf_rounded, m2m_ref):
    current = leaf_rounded
    for _ in range(LEVELS_DEV):
        count = current.shape[0] // 4
        total = jnp.zeros((count, current.shape[1]), F32)
        for child in range(4):
            total = total + matmul(
                current[child * count : (child + 1) * count].astype(BF16), m2m_ref[child]
            )
        current = rounded(total)
    return current


def prepare_kernel(
    positions_ref, strengths_ref, counts_ref, cross_ref, weights_ref, spread_ref, message_ref, low_ref, high_ref
):
    _, boxes, slots = positions_ref.shape
    entries = cross_ref.shape[1]
    cross = cross_ref[...]
    shift = slots.bit_length() - 1
    box_hit = iota((boxes, entries), 0) == lax.shift_right_logical(cross, shift)
    slot_hit = iota((slots, entries), 0) == (cross & (slots - 1))
    box_one = box_hit.astype(F32).astype(BF16)
    slot_one = slot_hit.astype(F32).astype(BF16)
    departed = matmul(box_one, slot_one, NT)
    square = (boxes, boxes)
    counts = jnp.sum(
        jnp.where(iota(square, 0) == iota(square, 1), counts_ref[...].astype(F32), 0.0), axis=1, keepdims=True
    )
    present = iota((boxes, slots), 1).astype(F32) < counts
    live = present & (departed < 0.5)
    for comp in range(3):
        weight = jnp.where(live, strengths_ref[comp], 0.0)
        weights_ref[comp] = weight
    spread_ref[...] = jnp.zeros_like(spread_ref)
    step = boxes // 4
    for first in range(step):
        slot = int(sum(((first >> (2 * d)) & 3) << (2 * (LEVELS_DEV - 1 - d)) for d in range(LEVELS_DEV)))
        for comp in range(3):
            rows = weights_ref[comp, pl.ds(first, 4, stride=step), :]
            spread_ref[pl.ds(slot * COMP_PAD + comp, 4, stride=COMP_PAD), :] = rows
    counted = jnp.sum(jnp.where(box_hit, counts, 0.0), axis=0, keepdims=True)
    leaves = (cross & (slots - 1)).astype(F32) < counted
    gathered = []
    for comp in range(6):
        value = positions_ref[comp] if comp < 3 else strengths_ref[comp - 3]
        high = rounded(value)
        both = jnp.concatenate([high, value - high], axis=1).astype(BF16)
        at_box = matmul(both, box_one, TN)
        picked = jnp.where(slot_hit, at_box[:slots] + at_box[slots:], 0.0)
        line = jnp.sum(picked, axis=0, keepdims=True)
        gathered.append(line if comp < 3 else jnp.where(leaves, line, 0.0))
    lines = jnp.concatenate(gathered, axis=0)
    high = rounded(lines)
    packed = jnp.concatenate([high, lines - high, jnp.zeros((4, entries), F32)], axis=0).astype(BF16)
    for comp in range(3):
        message_ref[comp * boxes : (comp + 1) * boxes, :] = positions_ref[comp].astype(BF16)
        message_ref[(3 + comp) * boxes : (4 + comp) * boxes, :] = weights_ref[comp].astype(BF16)
    for part in range(entries // slots):
        start = 6 * boxes + part * 16
        message_ref[start : start + 16, :] = packed[:, part * slots : (part + 1) * slots]
    pad = jnp.zeros((10, slots), F32)
    for ref, row in ((low_ref, 0), (high_ref, boxes - 1)):
        lines = [positions_ref[c, row : row + 1, :] for c in range(3)]
        lines += [weights_ref[c, row : row + 1, :] for c in range(3)]
        ref[...] = jnp.concatenate(lines + [pad], axis=0).astype(BF16)


def counts_kernel(source_ref, class_ref, out_ref):
    boxes, entries = source_ref.shape
    rows = boxes * COMP_PAD
    source = digit_reversed(source_ref[...])
    kind = class_ref[...]
    columns = iota((boxes, boxes), 1)
    totals = [jnp.zeros((boxes, boxes), F32) for _ in range(NCLASS)]
    for entry in range(entries):
        hit = source[:, entry : entry + 1] == columns
        for which in range(NCLASS):
            good = hit & (kind[:, entry : entry + 1] == which)
            totals[which] = totals[which] + good.astype(F32)
    left_box = digit_reversed(lax.shift_right_logical(iota((rows, boxes), 0), 2))
    left = (left_box == iota((rows, boxes), 1)).astype(F32).astype(BF16)
    right = (iota((boxes, rows), 0) == lax.shift_right_logical(iota((boxes, rows), 1), 2)).astype(F32).astype(BF16)
    same = (iota((rows, rows), 0) & 3) == (iota((rows, rows), 1) & 3)
    for which in range(NCLASS):
        spread = matmul(matmul(left, totals[which].astype(BF16)).astype(BF16), right)
        out_ref[which * rows : (which + 1) * rows, :] = jnp.where(same, spread, 0.0).astype(BF16)


def leaf_kernel(places_ref, spread_ref, leaf_ref, cheb_a_ref, cheb_b_ref):
    boxes = places_ref.shape[1]
    fill_chebyshev(cheb_a_ref, places_ref[0])
    fill_chebyshev(cheb_b_ref, places_ref[1])
    leaf_rows(cheb_a_ref, cheb_b_ref, spread_ref, leaf_ref, boxes)


def root_outputs(total, m2m_ref, multipole_ref, root_ref):
    spread = coefficient_spread(TERMS * TERMS, total.shape[1])
    leaf = matmul(total.astype(BF16), spread)
    multipole_ref[...] = leaf.astype(BF16)
    root = upward(leaf, m2m_ref)[:3].astype(BF16)
    root_ref[...] = jnp.broadcast_to(root[None], root_ref.shape)


def arrive_kernel(message_ref, arrive_ref, leaf_ref, m2m_ref, arrival_ref, multipole_ref, root_ref, *, start):
    rows, wide = leaf_ref.shape
    entries = arrive_ref.shape[1]
    slots = message_ref.shape[1]
    parts = []
    for part in range(entries // slots):
        parts.append(message_ref[start + part * 16 : start + part * 16 + 16, :].astype(F32))
    packed = jnp.concatenate(parts, axis=1)
    lines = packed[0:6] + packed[6:12]
    tail = [jnp.zeros((TERMS_PAD - TERMS, entries), F32)]
    cheb_a = jnp.concatenate(chebyshev_series(lines[0:1]) + tail, axis=0)
    cheb_b = jnp.concatenate(chebyshev_series(lines[1:2]) + tail, axis=0)
    terms = outer_terms(cheb_a, cheb_b)
    blank = jnp.zeros((1, entries), F32)
    eight = jnp.concatenate([lines[3:6], blank, lines[3:6], blank], axis=0)
    strength = jnp.broadcast_to(eight[None], (rows // 8, 8, entries)).reshape(rows, entries)
    landing = lax.shift_right_logical(iota((rows, entries), 0), 2) == digit_reversed(arrive_ref[...])
    placed = jnp.where(landing, strength, 0.0)
    high = placed.astype(BF16)
    low = (placed - high.astype(F32)).astype(BF16)
    arrival = matmul(high, terms, NT) + matmul(low, terms, NT)
    arrival_ref[...] = arrival
    root_outputs(leaf_ref[...] + arrival, m2m_ref, multipole_ref, root_ref)


def again_kernel(
    places_ref, spread_ref, arrival_ref, m2m_ref, multipole_ref, root_ref, cheb_a_ref, cheb_b_ref, leaf_ref
):
    leaf_kernel(places_ref, spread_ref, leaf_ref, cheb_a_ref, cheb_b_ref)
    root_outputs(leaf_ref[...] + arrival_ref[...], m2m_ref, multipole_ref, root_ref)


def near_kernel(
    places_ref,
    weights_ref,
    left_places_ref,
    right_places_ref,
    left_weights_ref,
    right_weights_ref,
    below_places_ref,
    above_places_ref,
    below_weights_ref,
    above_weights_ref,
    near_ref,
    source_ref,
    weight_ref,
    lines_ref,
    sums_ref,
):
    _, boxes, slots = places_ref.shape
    group = 8
    for comp in range(3):
        shift = [offset[comp] for offset in OFFSETS]
        own = places_ref[comp]
        mass = weights_ref[comp]
        rows = slice(comp * boxes, (comp + 1) * boxes)
        lifted = slice((3 + comp) * boxes, (4 + comp) * boxes)
        source_ref[0, comp] = own
        weight_ref[0, comp] = mass
        below = below_places_ref[...][comp : comp + 1].astype(F32)
        above = above_places_ref[...][comp : comp + 1].astype(F32)
        below_mass = below_weights_ref[...][3 + comp : 4 + comp].astype(F32)
        above_mass = above_weights_ref[...][3 + comp : 4 + comp].astype(F32)
        source_ref[1, comp] = jnp.concatenate([below, own[:-1]], axis=0) + shift[1]
        weight_ref[1, comp] = jnp.concatenate([below_mass, mass[:-1]], axis=0)
        source_ref[2, comp] = jnp.concatenate([own[1:], above], axis=0) + shift[2]
        weight_ref[2, comp] = jnp.concatenate([mass[1:], above_mass], axis=0)
        source_ref[3, comp] = left_places_ref[rows, :].astype(F32) + shift[3]
        weight_ref[3, comp] = left_weights_ref[lifted, :].astype(F32)
        source_ref[4, comp] = right_places_ref[rows, :].astype(F32) + shift[4]
        weight_ref[4, comp] = right_weights_ref[lifted, :].astype(F32)

    one = jnp.ones((group, slots), F32)
    zero = jnp.zeros((group, slots), F32)
    lane_row = iota((PIECES * group, slots), 0) & (group - 1)

    def thirds(value):
        first = rounded(value)
        second = rounded(value - first)
        return [first, second, value - first - second]

    def per_group(index, carry):
        rows = pl.ds(pl.multiple_of(index * group, group), group)
        target = []
        square = zero
        for comp in range(3):
            line = places_ref[comp, rows, :]
            first = rounded(line)
            target += [-2.0 * first, -2.0 * first, -2.0 * (line - first)]
            square = square + line * line
        target = jnp.concatenate(target + [one, one, one] + thirds(square) + [zero], axis=0).astype(BF16)
        columns = []
        for variant in range(5):
            source = []
            square = zero + DELTA_SQ
            place = [source_ref[variant, comp, rows, :] for comp in range(3)]
            mass = [weight_ref[variant, comp, rows, :] for comp in range(3)]
            for comp in range(3):
                first = rounded(place[comp])
                source += [first, place[comp] - first, first]
                square = square + place[comp] * place[comp]
            source = jnp.concatenate(source + thirds(square) + [one, one, one, zero], axis=0)
            columns.append(jnp.transpose(source).astype(BF16))
            moment = [
                mass[1] * place[2] - mass[2] * place[1],
                mass[2] * place[0] - mass[0] * place[2],
                mass[0] * place[1] - mass[1] * place[0],
            ]
            for comp, line in enumerate(mass + moment):
                high = rounded(line)
                lines_ref[variant, pl.ds(comp, group, stride=16), :] = high
                lines_ref[variant, pl.ds(8 + comp, group, stride=16), :] = line - high
        for first in range(0, group, 2):
            blocks = [jnp.where(lane_row == first + side, target, jnp.zeros_like(target)) for side in range(2)]
            grid = jnp.concatenate(blocks, axis=1)
            total = [jnp.zeros((16, slots), F32) for _ in range(2)]
            for variant in range(5):
                inverse = lax.rsqrt(matmul(columns[variant], grid))
                strength = (inverse * inverse * inverse).astype(BF16)
                for side in range(2):
                    mass = lines_ref[variant, (first + side) * 16 : (first + side + 1) * 16, :].astype(BF16)
                    total[side] = total[side] + matmul(mass, strength[:, side * slots : (side + 1) * slots])
            for side in range(2):
                sums_ref[pl.ds(pl.multiple_of((index * group + first + side) * 8, 8), 8), :] = (
                    total[side][:8] + total[side][8:]
                )
        return carry

    for variant in range(5):
        for blank in (6, 7, 14, 15):
            lines_ref[variant, pl.ds(blank, group, stride=16), :] = zero
    lax.fori_loop(0, boxes // group, per_group, 0)
    place = [places_ref[comp] for comp in range(3)]
    drift = [sums_ref[pl.ds(comp, boxes, stride=8), :] for comp in range(3)]
    moment = [sums_ref[pl.ds(3 + comp, boxes, stride=8), :] for comp in range(3)]
    near_ref[0] = INV_FOUR_PI * (drift[1] * place[2] - drift[2] * place[1] - moment[0])
    near_ref[1] = INV_FOUR_PI * (drift[2] * place[0] - drift[0] * place[2] - moment[1])
    near_ref[2] = INV_FOUR_PI * (drift[0] * place[1] - drift[1] * place[0] - moment[2])


def far_kernel(
    roots_ref,
    near_ref,
    places_ref,
    multipole_ref,
    pairs_ref,
    m2m_ref,
    m2l_leaf_ref,
    tree_up_ref,
    tree_m2l_ref,
    m2l_sector_ref,
    velocity_ref,
    moved_ref,
    *rest,
    sectors,
    groups,
):
    *messages, nodes_ref, cheb_a_ref, cheb_b_ref, local_ref, far_ref = rest
    _, boxes, slots = places_ref.shape
    coef = TERMS * TERMS
    depth = groups.bit_length() - 1
    sector = lax.axis_index("sector")
    block = lax.axis_index("box")
    order = [int(format(n, "b").zfill(depth)[::-1], 2) if depth else 0 for n in range(groups)]
    nodes = jnp.concatenate(
        [roots_ref[s * groups + order[n]].astype(F32) for n in range(groups) for s in range(sectors)], axis=0
    )
    base = [0]
    for level in range(depth + 1):
        count = nodes.shape[0] // 3
        for n in range(count):
            nodes_ref[base[level] + n, 0:3, :] = nodes[3 * n : 3 * n + 3]
        base.append(base[level] + count)
        if level < depth:
            half = nodes.shape[0] // 2
            nodes = rounded(
                matmul(nodes[:half].astype(BF16), tree_up_ref[0]) + matmul(nodes[half:].astype(BF16), tree_up_ref[1])
            )
    local = jnp.zeros((3, coef), F32)
    for ahead in range(1, sectors):
        other = lax.rem(sector + ahead, sectors)
        local = local + matmul(nodes_ref[base[depth] + other][:3].astype(BF16), m2l_sector_ref[ahead - 1])
    local = local.astype(BF16)
    for level in reversed(range(depth)):
        node = lax.shift_right_logical(block, level)
        side = node & 1
        node = node ^ 1
        place = node & 1
        for bit in range(1, depth - level):
            place = place * 2 + (lax.shift_right_logical(node, bit) & 1)
        sibling = nodes_ref[base[level] + place * sectors + sector][:3].astype(BF16)
        local = (matmul(local, tree_up_ref[side], NT) + matmul(sibling, tree_m2l_ref[side])).astype(BF16)
    current = jnp.concatenate([local.astype(F32), jnp.zeros((COMP_PAD - 3, coef), F32)], axis=0)
    for level in range(LEVELS_DEV):
        parent = current.astype(BF16)
        current = jnp.concatenate([matmul(parent, m2m_ref[child], NT) for child in range(4)], axis=0)
    rows = boxes * COMP_PAD
    for which in range(NCLASS):
        presum = matmul(pairs_ref[which * rows : (which + 1) * rows, :], multipole_ref[...]).astype(BF16)
        current = current + matmul(presum, m2l_leaf_ref[which])
    wide = local_ref.shape[2]
    spread = coefficient_spread(coef, wide)
    high = rounded(current)
    local_ref[0] = matmul(high.astype(BF16), spread, NT)
    local_ref[1] = matmul((current - high).astype(BF16), spread, NT)
    fill_chebyshev(cheb_a_ref, places_ref[0])
    fill_chebyshev(cheb_b_ref, places_ref[1])

    def pair(index, carry):
        group = pl.ds(pl.multiple_of(index * 8, 8), 8)
        local = jnp.concatenate([local_ref[0, group, :], local_ref[1, group, :]], axis=0).astype(BF16)
        for half in range(2):
            box = digit_reversed(index * 2 + half)
            both = matmul(local, box_terms(cheb_a_ref, cheb_b_ref, box, boxes))
            far_ref[pl.ds(pl.multiple_of(box * 8, 8), 8), :] = both[:8] + both[8:]
        return carry

    lax.fori_loop(0, boxes // 2, pair, 0, unroll=2)
    run = boxes // 4
    speed = []
    for comp in range(3):
        parts = []
        for digit in range(4):
            start = digit * run * 8 + (digit % 2) * COMP_PAD + comp
            parts.append(far_ref[pl.ds(start, run, stride=8), :])
        velocity = near_ref[comp] + jnp.concatenate(parts, axis=0) / TERMS
        velocity_ref[comp] = velocity
        moved = places_ref[comp] + TIME_STEP * velocity
        moved_ref[comp] = moved
        speed.append(moved)
    if messages:
        message_ref, low_ref, high_ref = messages
        for comp in range(3):
            message_ref[comp * boxes : (comp + 1) * boxes, :] = speed[comp].astype(BF16)
        pad = jnp.zeros((13, slots), F32)
        low_ref[...] = jnp.concatenate([m[:1] for m in speed] + [pad], axis=0).astype(BF16)
        high_ref[...] = jnp.concatenate([m[-1:] for m in speed] + [pad], axis=0).astype(BF16)


def halo(message, low, high):
    sectors, groups = lax.axis_size("sector"), lax.axis_size("box")
    up = [(i, (i + 1) % sectors) for i in range(sectors)]
    down = [(j, i) for i, j in up]
    along = [(i, i + 1) for i in range(groups - 1)]
    back = [(j, i) for i, j in along]
    return (
        lax.ppermute(message, "sector", up),
        lax.ppermute(message, "sector", down),
        lax.ppermute(high, "box", along),
        lax.ppermute(low, "box", back),
    )


def per_device(
    positions,
    strengths,
    counts,
    cross_slot,
    arrive_box,
    il_source,
    il_class,
    m2m,
    m2l_leaf,
    tree_up,
    tree_m2l,
    m2l_sector,
):
    sectors, groups = lax.axis_size("sector"), lax.axis_size("box")
    devices = sectors * groups
    _, _, boxes, slots = positions.shape
    entries = cross_slot.shape[1]
    coef = m2m.shape[-1]
    wide = -(-TERMS * TERMS_PAD // 128) * 128
    rows = boxes * COMP_PAD
    field = jax.ShapeDtypeStruct((3, boxes, slots), F32)
    edge = jax.ShapeDtypeStruct((16, slots), BF16)
    leaf_shape = jax.ShapeDtypeStruct((rows, wide), F32)
    multipole_shape = jax.ShapeDtypeStruct((rows, coef), BF16)
    root_shape = jax.ShapeDtypeStruct((devices, 3, coef), BF16)
    cheb = pltpu.VMEM((TERMS_PAD * boxes, slots), F32)

    def call(body, out_shape, scratch=(), name=None, **keys):
        return pl.pallas_call(
            functools.partial(body, **keys) if keys else body,
            out_shape=out_shape,
            scratch_shapes=list(scratch),
            name=name,
        )

    places = positions.reshape(3, boxes, slots)
    weights, spread, message, low, high = call(
        prepare_kernel,
        (
            field,
            jax.ShapeDtypeStruct((rows, slots), F32),
            jax.ShapeDtypeStruct((6 * boxes + entries // slots * 16, slots), BF16),
            edge,
            edge,
        ),
        name="prepare",
    )(places, strengths.reshape(3, boxes, slots), counts, cross_slot)
    left, right, below, above = halo(message, low, high)
    pairs = call(counts_kernel, jax.ShapeDtypeStruct((NCLASS * rows, rows), BF16), name="pair_counts")(
        il_source.reshape(boxes, -1), il_class.reshape(boxes, -1)
    )
    leaf = call(leaf_kernel, leaf_shape, (cheb, cheb), name="leaf")(places, spread)
    arrival, multipole, root = call(
        arrive_kernel, (leaf_shape, multipole_shape, root_shape), name="arrive", start=6 * boxes
    )(left, arrive_box, leaf, m2m)
    halo_weights = (left, right)
    edge_weights = (below, above)
    halo_places = (left, right)
    edge_places = (below, above)
    velocity = None
    for substep in range(2):
        if substep:
            multipole, root = call(
                again_kernel,
                (multipole_shape, root_shape),
                (cheb, cheb, pltpu.VMEM((rows, wide), F32)),
                name="again",
            )(places, spread, arrival, m2m)
        roots = lax.all_to_all(root, ("sector", "box"), 0, 0, tiled=True)
        near = call(
            near_kernel,
            field,
            (
                pltpu.VMEM((5, 3, boxes, slots), F32),
                pltpu.VMEM((5, 3, boxes, slots), F32),
                pltpu.VMEM((5, 8 * 16, slots), F32),
                pltpu.VMEM((boxes * 8, slots), F32),
            ),
            name="near",
        )(places, weights, *halo_places, *halo_weights, *edge_places, *edge_weights)
        extra = ()
        if substep == 0:
            extra = (jax.ShapeDtypeStruct((3 * boxes, slots), BF16), edge, edge)
        velocity, places, *sent = call(
            far_kernel,
            (field, field) + extra,
            (
                pltpu.VMEM((2 * devices, 8, coef), F32),
                cheb,
                cheb,
                pltpu.VMEM((2, rows, wide), F32),
                pltpu.VMEM((boxes * 8, slots), F32),
            ),
            name="far",
            sectors=sectors,
            groups=groups,
        )(roots, near, places, multipole, pairs, m2m, m2l_leaf, tree_up, tree_m2l, m2l_sector)
        if substep == 0:
            left, right, below, above = halo(*sent)
            halo_places = (left, right)
            edge_places = (below, above)
    return (places[:, None], velocity[:, None])


def solution(mesh):
    placed = (
        P(None, "sector", "box", None),
        P(None, "sector", "box", None),
        P("sector", "box"),
        P("sector", "box"),
        P("sector", "box"),
        P("sector", "box", None),
        P("sector", "box", None),
        P(),
        P(),
        P(),
        P(),
        P(),
    )
    return jax.shard_map(
        per_device,
        mesh=mesh,
        in_specs=placed,
        out_specs=(P(None, "sector", "box", None), P(None, "sector", "box", None)),
        check_vma=False,
    )
```

time: 353 us -> 147 us (0.42)
  other arithmetic: 144 us -> 0 us
  Pallas kernels: 0 us -> 103 us
  local copies, waits for them, and re-layouts: 85.4 us -> 12.1 us
  matrix products: 71.1 us -> 0 us
  blocking collectives: 17.3 us -> 0 us
    reduce_sum x4 -> x0, other arithmetic: 109 us -> none  [pair_velocity(): jnp.sum(inverse * (weight_y * delta_z - weight_z * delta_y), axis=2)]
    pallas_call x0 -> x9, Pallas kernels: none -> 103 us  [the longest x2 52.4 us: per_device(): call(near_kernel, field, (pltpu.VMEM((5, 3, boxes, slots), F32), pltpu.VM...]
    dot_general x38 -> x0, matrix products: 71.1 us -> none  [the longest x6 13.6 us: far_field(): jnp.einsum('cy,xy->cx', local, up_side, preferred_element_type=jnp.float32)]
    reshape x13 -> x0, local copies, waits for them, and re-layouts: 22.6 us -> none  [the longest x4 10.6 us: far_field(): presum = presum.astype(jnp.bfloat16).reshape(NCLASS, box_count * 3, coef)]
    all_gather x2 -> x0, blocking collectives: 17.3 us -> none  [far_field(): piece = lax.all_gather(current[None], 'sector', axis=0, tiled=True)]
    convert_element_type x10 -> x0, local copies, waits for them, and re-layouts: 16.7 us -> none  [the longest x6 14.5 us: far_field(): leaf = (multipoles(cheb_a, cheb_b, weights) + arrival_terms).reshape(box_...]
    unnamed x105 -> x0, other arithmetic: 14.2 us -> none
    all_to_all x0 -> x2, starting transfers between devices: none -> 11.2 us  [per_device(): roots = lax.all_to_all(root, ('sector', 'box'), 0, 0, tiled=True)]
  transfers between devices with their start and end apart: 15 -> 10, of which waited for: 1 -> 1; matrix products, arithmetic and copies ran while one was open for 61% -> 6% of each run, Pallas kernels for 0% -> 43%
where the time goes in v1:
time: 147 us; the launch traced here: 144 us
  Pallas kernels  103 us (70%)
  starting transfers between devices  25.8 us (18%)
  local copies, waits for them, and re-layouts  12.1 us (8%)
  waiting for transfers between devices  2.84 us (2%)
    pallas_call x2, Pallas kernels, per_device(): call(near_kernel, field, (pltpu.VMEM((5, 3, boxes, slots), F32), pltpu.VM...  52.4 us
    pallas_call x2, Pallas kernels, per_device(): call(far_kernel, (field, field) + extra, (pltpu.VMEM((2 * devices, 8, coe...  26.6 us
    unnamed x48, local copies, waits for them, and re-layouts  12.1 us
    all_to_all x2, starting transfers between devices, per_device(): roots = lax.all_to_all(root, ('sector', 'box'), 0, 0, tiled=True)  11.2 us
    pallas_call x1, Pallas kernels, per_device(): call(again_kernel, (multipole_shape, root_shape), (cheb, cheb, pltpu.VMEM...  8.51 us
    pallas_call x1, Pallas kernels, per_device(): call(leaf_kernel, leaf_shape, (cheb, cheb), name='leaf')(places, spread)  6.49 us
    ppermute x2, starting transfers between devices, halo(): lax.ppermute(message, 'sector', down)  5.44 us
    pallas_call x1, Pallas kernels, per_device(): call(arrive_kernel, (leaf_shape, multipole_shape, root_shape), name='arri...  4 us
  transfers between devices with their start and end apart: 10, of which 1 were waited for; matrix products, arithmetic and copies ran while one was open for 6% of the time, Pallas kernels for 43%

profile of v1, /device:TPU:0, one launch (start us, length us, event | category | flops | bytes accessed | tf_op | source)
XLA Modules:
  0.0 144.4 jit_solution(1313158515982831132)
XLA Ops:
  0.6 2.1 %prepare.1 = (f32[3,64,128]{2,1,0:T(8,128)}, f32[256,128]{1,0:T(8,128)}, bf16[416,128]{1,0:T(8,128)(2,1)}, bf16[16,128]{1,0:T(8,128)(2,1)}, bf16[16,128]{1,0:T(8,128)(2,1)}) custom-call(f32[3,64,128]{2,1,0:T(8,128)} %bitcast.10, f32[3,64,128]{2,1,0:T(8,128)} %bitcast.16, s32[1,64]{1,0:T(1,128)} %counts_ref.1, s32[1,256]{1,0:T(1,128)} %cross_ref.1), custom_call_target="tpu_custom_call" | custom-call | tf_op jit(solution)/shard_map/prepare/pallas_call | solution.py:497
  2.7 3.0 %collective-permute-start = (bf16[416,128]{1,0:T(8,128)(2,1)}, bf16[416,128]{1,0:T(8,128)(2,1)S(1)}, u32[]{:S(2)}, u32[]{:S(2)}) collective-permute-start(bf16[416,128]{1,0:T(8,128)(2,1)} %get-tuple-element.18), channel_id=1, source_target_pairs={{0,8},{8,16},{16,24},{24,0},{1,9},{9,17},{17,25},{25,1},{2,10},{10... | collective-permute-start | bytes 319496 | tf_op jit(solution)/shard_map/ppermute | solution.py:453
  5.7 6.5 %leaf.1.leaf_ref = f32[256,512]{1,0:T(8,128)} custom-call(f32[3,64,128]{2,1,0:T(8,128)} %bitcast.11, f32[256,128]{1,0:T(8,128)} %get-tuple-element.19.spread_ref), custom_call_target="tpu_custom_call" | custom-call | tf_op jit(solution)/shard_map/leaf/pallas_call | solution.py:512
  12.1 3.1 %copy.14.m2m_ref = bf16[4,441,441]{2,1,0:T(8,128)(2,1)} copy(bf16[4,441,441]{2,0,1:T(4,128)(2,1)} %param.19) | data formatting | bytes 3111696 | tf_op args[7]
  15.9 4.0 %arrive.1 = (f32[256,512]{1,0:T(8,128)}, bf16[256,441]{1,0:T(8,128)(2,1)}, bf16[32,3,441]{2,1,0:T(4,128)(2,1)}) custom-call(bf16[416,128]{1,0:T(8,128)(2,1)} %copy-done.1, s32[1,256]{1,0:T(1,128)} %arrive_ref.1, f32[256,512]{1,0:T(8,128)} %leaf.1.leaf_ref, bf16[4,441,441]{2,1,0:T(8,128)(2,1)} %copy.14.m2m_ref), custom_call_target="tpu_custom_call" | custom-call | tf_op jit(solution)/shard_map/arrive/pallas_call | solution.py:513
  19.9 4.9 %all-to-all-start = ((bf16[32,3,441]{2,1,0:T(4,128)(2,1)}), bf16[32,3,441]{2,1,0:T(4,128)(2,1)S(1)}, u32[]{:S(2)}, u32[]{:S(2)}) async-start(bf16[32,3,441]{2,1,0:T(4,128)(2,1)} %get-tuple-element.20), calls=%async_computation | async-start | bytes 262144 | tf_op jit(solution)/shard_map/all_to_all | solution.py:529
  24.9 2.7 %collective-permute-start.1 = (bf16[416,128]{1,0:T(8,128)(2,1)S(1)}, bf16[416,128]{1,0:T(8,128)(2,1)S(1)}, u32[]{:S(2)}, u32[]{:S(2)}) collective-permute-start(bf16[416,128]{1,0:T(8,128)(2,1)S(1)} %copy-done.15), channel_id=1, source_target_pairs={{8,0},{16,8},{24,16},{0,24},{9,1},{17,9},{25,17},{1,25},{10,2},{18... | collective-permute-start | bytes 319496 | tf_op jit(solution)/shard_map/ppermute | solution.py:454
  27.6 1.7 %collective-permute-start.2 = (bf16[16,128]{1,0:T(8,128)(2,1)S(1)}, bf16[16,128]{1,0:T(8,128)(2,1)S(1)}, u32[]{:S(2)}, u32[]{:S(2)}) collective-permute-start(bf16[16,128]{1,0:T(8,128)(2,1)S(1)} %copy-done.18), channel_id=1, source_target_pairs={{0,1},{1,2},{2,3},{3,4},{4,5},{5,6},{6,7},{8,9},{9,10},{10,11},{11... | collective-permute-start | bytes 12296 | tf_op jit(solution)/shard_map/ppermute | solution.py:455
  29.3 1.3 collective-permute-start.3
  31.4 0.7 copy.16
  32.1 1.1 copy.19.tree_up_ref
  33.1 1.1 copy.20.tree_m2l_ref
  34.2 1.6 %copy.18.m2l_leaf_ref = bf16[4,441,441]{2,1,0:T(8,128)(2,1)} copy(bf16[4,441,441]{2,0,1:T(4,128)(2,1)S(1)} %copy-done) | data formatting | bytes 3111696 | tf_op args[8]
  35.8 2.8 %pair_counts.1.pairs_ref = bf16[1024,256]{1,0:T(8,128)(2,1)} custom-call(s32[64,16]{1,0:T(8,128)} %bitcast.14, s32[64,16]{1,0:T(8,128)} %bitcast.15), custom_call_target="tpu_custom_call" | custom-call | tf_op jit(solution)/shard_map/pair_counts/pallas_call | solution.py:509
  39.3 26.2 %near.2.near_ref = f32[3,64,128]{2,1,0:T(8,128)} custom-call(f32[3,64,128]{2,1,0:T(8,128)} %bitcast.12, f32[3,64,128]{2,1,0:T(8,128)} %get-tuple-element.21.weights_ref, bf16[416,128]{1,0:T(8,128)(2,1)} %copy-done.1, bf16[416,128]{1,0:T(8,128)(2,1)} %copy-done.2, bf16[416,128]{1,0:T(8,128)(2,1)} %copy-done.1, bf16[416,128]{1,0:T(8,128)(2,1)} %copy-done.2, ...), custom_call_target="tpu_custom_call" | custom-call | tf_op jit(solution)/shard_map/near/pallas_call | solution.py:530
  66.2 13.3 %far.2 = (f32[3,64,128]{2,1,0:T(8,128)}, f32[3,64,128]{2,1,0:T(8,128)}, bf16[192,128]{1,0:T(8,128)(2,1)}, bf16[16,128]{1,0:T(8,128)(2,1)}, bf16[16,128]{1,0:T(8,128)(2,1)}) custom-call(bf16[32,3,441]{2,1,0:T(4,128)(2,1)} %copy-done.6, f32[3,64,128]{2,1,0:T(8,128)} %near.2.near_ref, f32[3,64,128]{2,1,0:T(8,128)} %bitcast.13, ...), custom_call_target="tpu_custom_call" | custom-call | tf_op jit(solution)/shard_map/far/pallas_call | solution.py:544
  79.5 8.5 %again.1 = (bf16[256,441]{1,0:T(8,128)(2,1)}, bf16[32,3,441]{2,1,0:T(4,128)(2,1)}) custom-call(f32[3,64,128]{2,1,0:T(8,128)} %get-tuple-element.25.places_ref, f32[256,128]{1,0:T(8,128)} %get-tuple-element.19.spread_ref, f32[256,512]{1,0:T(8,128)} %get-tuple-element.26.arrival_ref, bf16[4,441,441]{2,1,0:T(8,128)(2,1)} %copy.14.m2m_ref), custom_call_target="tpu_custom_call" | custom-call | tf_op jit(solution)/shard_map/again/pallas_call | solution.py:523
  88.0 6.3 %all-to-all-start.1 = ((bf16[32,3,441]{2,1,0:T(4,128)(2,1)}), bf16[32,3,441]{2,1,0:T(4,128)(2,1)S(1)}, u32[]{:S(2)}, u32[]{:S(2)}) async-start(bf16[32,3,441]{2,1,0:T(4,128)(2,1)} %get-tuple-element.27), calls=%async_computation.1 | async-start | bytes 262144 | tf_op jit(solution)/shard_map/all_to_all | solution.py:529
  94.3 2.7 %collective-permute-start.5 = (bf16[192,128]{1,0:T(8,128)(2,1)S(1)}, bf16[192,128]{1,0:T(8,128)(2,1)S(1)}, u32[]{:S(2)}, u32[]{:S(2)}) collective-permute-start(bf16[192,128]{1,0:T(8,128)(2,1)S(1)} %copy-done.16), channel_id=1, source_target_pairs={{8,0},{16,8},{24,16},{0,24},{9,1},{17,9},{25,17},{1,25},{10,2},{18... | collective-permute-start | bytes 147464 | tf_op jit(solution)/shard_map/ppermute | solution.py:454
  97.0 1.7 %collective-permute-start.6 = (bf16[16,128]{1,0:T(8,128)(2,1)S(1)}, bf16[16,128]{1,0:T(8,128)(2,1)S(1)}, u32[]{:S(2)}, u32[]{:S(2)}) collective-permute-start(bf16[16,128]{1,0:T(8,128)(2,1)S(1)} %copy-done.20), channel_id=1, source_target_pairs={{0,1},{1,2},{2,3},{3,4},{4,5},{5,6},{6,7},{8,9},{9,10},{10,11},{11... | collective-permute-start | bytes 12296 | tf_op jit(solution)/shard_map/ppermute | solution.py:455
  98.8 1.5 %collective-permute-start.7 = (bf16[16,128]{1,0:T(8,128)(2,1)S(1)}, bf16[16,128]{1,0:T(8,128)(2,1)S(1)}, u32[]{:S(2)}, u32[]{:S(2)}) collective-permute-start(bf16[16,128]{1,0:T(8,128)(2,1)S(1)} %copy-done.19), channel_id=1, source_target_pairs={{1,0},{2,1},{3,2},{4,3},{5,4},{6,5},{7,6},{9,8},{10,9},{11,10},{12... | collective-permute-start | bytes 12296 | tf_op jit(solution)/shard_map/ppermute | solution.py:456
  100.3 2.8 %collective-permute-done.7.above_places_ref = bf16[16,128]{1,0:T(8,128)(2,1)S(1)} collective-permute-done((bf16[16,128]{1,0:T(8,128)(2,1)S(1)}, bf16[16,128]{1,0:T(8,128)(2,1)S(1)}, u32[]{:S(2)}, u32[]{:S(2)}) %collective-permute-start.7) | collective-permute-done | bytes 4128 | tf_op jit(solution)/shard_map/ppermute | solution.py:456
  104.3 26.2 %near.3.near_ref = f32[3,64,128]{2,1,0:T(8,128)} custom-call(f32[3,64,128]{2,1,0:T(8,128)} %get-tuple-element.25.places_ref, f32[3,64,128]{2,1,0:T(8,128)} %get-tuple-element.21.weights_ref, bf16[192,128]{1,0:T(8,128)(2,1)} %copy-done.8, bf16[192,128]{1,0:T(8,128)(2,1)} %copy-done.7, bf16[416,128]{1,0:T(8,128)(2,1)} %copy-done.1, ...), custom_call_target="tpu_custom_call" | custom-call | tf_op jit(solution)/shard_map/near/pallas_call | solution.py:530
  131.2 13.3 %far.3 = (f32[3,64,128]{2,1,0:T(8,128)}, f32[3,64,128]{2,1,0:T(8,128)}) custom-call(bf16[32,3,441]{2,1,0:T(4,128)(2,1)} %copy-done.5, f32[3,64,128]{2,1,0:T(8,128)} %near.3.near_ref, f32[3,64,128]{2,1,0:T(8,128)} %get-tuple-element.25.places_ref, bf16[256,441]{1,0:T(8,128)(2,1)} %get-tuple-element.31.multipole_ref, bf16[1024,256]{1,0:T(8,128)(2,1)} %pair_counts.1.pairs_ref, ...), custom_call_target="tpu_custom_call" | custom-call | tf_op jit(solution)/shard_map/far/pallas_call | solution.py:544
  (53 shorter events, 4.6 us)
Async XLA Ops:
  2.7 12.6 %collective-permute-start = (bf16[416,128]{1,0:T(8,128)(2,1)}, bf16[416,128]{1,0:T(8,128)(2,1)S(1)}, u32[]{:S(2)}, u32[]{:S(2)}) collective-permute-start(bf16[416,128]{1,0:T(8,128)(2,1)} %get-tuple-element.18), channel_id=1, source_target_pairs={{0,8},{8,16},{16,24},{24,0},{1,9},{9,17},{17,25},{25,1},{2,10},{10... | collective-permute-start | bytes 319496 | tf_op jit(solution)/shard_map/ppermute | solution.py:453
  15.2 9.6 %copy-start.15 = (bf16[416,128]{1,0:T(8,128)(2,1)S(1)}, bf16[416,128]{1,0:T(8,128)(2,1)}, u32[]{:S(2)}) copy-start(bf16[416,128]{1,0:T(8,128)(2,1)} %get-tuple-element.18) | copy-start | bytes 319492
  15.2 12.4 %copy-start.18 = (bf16[16,128]{1,0:T(8,128)(2,1)S(1)}, bf16[16,128]{1,0:T(8,128)(2,1)}, u32[]{:S(2)}) copy-start(bf16[16,128]{1,0:T(8,128)(2,1)} %get-tuple-element.22) | copy-start | bytes 12292
  15.2 14.1 %copy-start.17 = (bf16[16,128]{1,0:T(8,128)(2,1)S(1)}, bf16[16,128]{1,0:T(8,128)(2,1)}, u32[]{:S(2)}) copy-start(bf16[16,128]{1,0:T(8,128)(2,1)} %get-tuple-element.23) | copy-start | bytes 12292
  15.2 15.4 %copy-start.11 = (s32[1,64,16]{1,2,0:T(8,128)S(1)}, s32[1,64,16]{1,2,0:T(8,128)}, u32[]{:S(2)}) copy-start(s32[1,64,16]{1,2,0:T(8,128)} %param.17) | copy-start | bytes 12292
  15.2 16.1 %copy-start.12 = (s32[1,64,16]{1,2,0:T(8,128)S(1)}, s32[1,64,16]{1,2,0:T(8,128)}, u32[]{:S(2)}) copy-start(s32[1,64,16]{1,2,0:T(8,128)} %param.18) | copy-start | bytes 12292
  15.2 16.8 %copy-start.3 = (bf16[2,441,441]{2,0,1:T(2,128)(2,1)S(1)}, bf16[2,441,441]{2,0,1:T(2,128)(2,1)}, u32[]{:S(2)}) copy-start(bf16[2,441,441]{2,0,1:T(2,128)(2,1)} %param.21) | copy-start | bytes 2333776
  15.3 17.9 %copy-start.4 = (bf16[2,441,441]{2,0,1:T(2,128)(2,1)S(1)}, bf16[2,441,441]{2,0,1:T(2,128)(2,1)}, u32[]{:S(2)}) copy-start(bf16[2,441,441]{2,0,1:T(2,128)(2,1)} %param.22) | copy-start | bytes 2333776
  19.9 45.6 %all-to-all-start = ((bf16[32,3,441]{2,1,0:T(4,128)(2,1)}), bf16[32,3,441]{2,1,0:T(4,128)(2,1)S(1)}, u32[]{:S(2)}, u32[]{:S(2)}) async-start(bf16[32,3,441]{2,1,0:T(4,128)(2,1)} %get-tuple-element.20), calls=%async_computation | async-start | bytes 262144 | tf_op jit(solution)/shard_map/all_to_all | solution.py:529
  24.9 13.8 %collective-permute-start.1 = (bf16[416,128]{1,0:T(8,128)(2,1)S(1)}, bf16[416,128]{1,0:T(8,128)(2,1)S(1)}, u32[]{:S(2)}, u32[]{:S(2)}) collective-permute-start(bf16[416,128]{1,0:T(8,128)(2,1)S(1)} %copy-done.15), channel_id=1, source_target_pairs={{8,0},{16,8},{24,16},{0,24},{9,1},{17,9},{25,17},{1,25},{10,2},{18... | collective-permute-start | bytes 319496 | tf_op jit(solution)/shard_map/ppermute | solution.py:454
  27.6 11.1 %collective-permute-start.2 = (bf16[16,128]{1,0:T(8,128)(2,1)S(1)}, bf16[16,128]{1,0:T(8,128)(2,1)S(1)}, u32[]{:S(2)}, u32[]{:S(2)}) collective-permute-start(bf16[16,128]{1,0:T(8,128)(2,1)S(1)} %copy-done.18), channel_id=1, source_target_pairs={{0,1},{1,2},{2,3},{3,4},{4,5},{5,6},{6,7},{8,9},{9,10},{10,11},{11... | collective-permute-start | bytes 12296 | tf_op jit(solution)/shard_map/ppermute | solution.py:455
  29.3 9.3 %collective-permute-start.3 = (bf16[16,128]{1,0:T(8,128)(2,1)S(1)}, bf16[16,128]{1,0:T(8,128)(2,1)S(1)}, u32[]{:S(2)}, u32[]{:S(2)}) collective-permute-start(bf16[16,128]{1,0:T(8,128)(2,1)S(1)} %copy-done.17), channel_id=1, source_target_pairs={{1,0},{2,1},{3,2},{4,3},{5,4},{6,5},{7,6},{9,8},{10,9},{11,10},{12... | collective-permute-start | bytes 12296 | tf_op jit(solution)/shard_map/ppermute | solution.py:456
  32.1 2.2 %copy-start = (bf16[4,441,441]{2,0,1:T(4,128)(2,1)S(1)}, bf16[4,441,441]{2,0,1:T(4,128)(2,1)}, u32[]{:S(2)}) copy-start(bf16[4,441,441]{2,0,1:T(4,128)(2,1)} %param.20) | copy-start | bytes 4667548
  38.7 0.7 copy-start.2
  65.5 0.7 copy-start.6
  79.5 14.8 %copy-start.16 = (bf16[192,128]{1,0:T(8,128)(2,1)S(1)}, bf16[192,128]{1,0:T(8,128)(2,1)}, u32[]{:S(2)}) copy-start(bf16[192,128]{1,0:T(8,128)(2,1)} %get-tuple-element.28) | copy-start | bytes 147460
  79.5 17.5 %copy-start.20 = (bf16[16,128]{1,0:T(8,128)(2,1)S(1)}, bf16[16,128]{1,0:T(8,128)(2,1)}, u32[]{:S(2)}) copy-start(bf16[16,128]{1,0:T(8,128)(2,1)} %get-tuple-element.29) | copy-start | bytes 12292
  79.5 19.3 %copy-start.19 = (bf16[16,128]{1,0:T(8,128)(2,1)S(1)}, bf16[16,128]{1,0:T(8,128)(2,1)}, u32[]{:S(2)}) copy-start(bf16[16,128]{1,0:T(8,128)(2,1)} %get-tuple-element.30) | copy-start | bytes 12292
  88.0 42.5 %all-to-all-start.1 = ((bf16[32,3,441]{2,1,0:T(4,128)(2,1)}), bf16[32,3,441]{2,1,0:T(4,128)(2,1)S(1)}, u32[]{:S(2)}, u32[]{:S(2)}) async-start(bf16[32,3,441]{2,1,0:T(4,128)(2,1)} %get-tuple-element.27), calls=%async_computation.1 | async-start | bytes 262144 | tf_op jit(solution)/shard_map/all_to_all | solution.py:529
  94.3 8.8 %collective-permute-start.5 = (bf16[192,128]{1,0:T(8,128)(2,1)S(1)}, bf16[192,128]{1,0:T(8,128)(2,1)S(1)}, u32[]{:S(2)}, u32[]{:S(2)}) collective-permute-start(bf16[192,128]{1,0:T(8,128)(2,1)S(1)} %copy-done.16), channel_id=1, source_target_pairs={{8,0},{16,8},{24,16},{0,24},{9,1},{17,9},{25,17},{1,25},{10,2},{18... | collective-permute-start | bytes 147464 | tf_op jit(solution)/shard_map/ppermute | solution.py:454
  97.0 6.1 %collective-permute-start.4 = (bf16[192,128]{1,0:T(8,128)(2,1)S(1)}, bf16[192,128]{1,0:T(8,128)(2,1)S(1)}, u32[]{:S(2)}, u32[]{:S(2)}) collective-permute-start(bf16[192,128]{1,0:T(8,128)(2,1)S(1)} %copy-done.16), channel_id=1, source_target_pairs={{0,8},{8,16},{16,24},{24,0},{1,9},{9,17},{17,25},{25,1},{2,10},{10... | collective-permute-start | bytes 147464 | tf_op jit(solution)/shard_map/ppermute | solution.py:453
  97.0 3.2 %collective-permute-start.6 = (bf16[16,128]{1,0:T(8,128)(2,1)S(1)}, bf16[16,128]{1,0:T(8,128)(2,1)S(1)}, u32[]{:S(2)}, u32[]{:S(2)}) collective-permute-start(bf16[16,128]{1,0:T(8,128)(2,1)S(1)} %copy-done.20), channel_id=1, source_target_pairs={{0,1},{1,2},{2,3},{3,4},{4,5},{5,6},{6,7},{8,9},{9,10},{10,11},{11... | collective-permute-start | bytes 12296 | tf_op jit(solution)/shard_map/ppermute | solution.py:455
  98.8 4.3 %collective-permute-start.7 = (bf16[16,128]{1,0:T(8,128)(2,1)S(1)}, bf16[16,128]{1,0:T(8,128)(2,1)S(1)}, u32[]{:S(2)}, u32[]{:S(2)}) collective-permute-start(bf16[16,128]{1,0:T(8,128)(2,1)S(1)} %copy-done.19), channel_id=1, source_target_pairs={{1,0},{2,1},{3,2},{4,3},{5,4},{6,5},{7,6},{9,8},{10,9},{11,10},{12... | collective-permute-start | bytes 12296 | tf_op jit(solution)/shard_map/ppermute | solution.py:456
  100.3 2.8 %copy-start.13 = (bf16[16,128]{1,0:T(8,128)(2,1)}, bf16[16,128]{1,0:T(8,128)(2,1)S(1)}, u32[]{:S(2)}) copy-start(bf16[16,128]{1,0:T(8,128)(2,1)S(1)} %collective-permute-done.6.below_places_ref) | copy-start | bytes 12292
  (7 other events, 4.3 us)
